TPU v7x, 256 devices: a whole 4x4x8 slice. The times are simulated.
256 devices in a mesh: ctx: 32 (over z, x_hi, core), tp: 8 (over y, x_lo).
Axes of the slice: x: 4 (x_hi: 2, x_lo: 2; x = x_hi * 2 + x_lo), y: 4, z: 8, core: 2. Of those that a mesh axis runs over, the one named last changes fastest.
Arguments:
- token_ids: int32 [4096], P('ctx'), may hold values from 0 to 511
- stream_table: bfloat16 [3, 512, 4096], P(None, None, 'tp'), may hold values from -6 to 6
- filters: float32 [256, 128], P('tp'), may hold values from -4 to 4
- proj_qk: bfloat16 [4096, 2, 4096], P(None, None, 'tp'), may hold values from -4 to 4
Outputs:
- attended: bfloat16 [4096, 4096], P('ctx', 'tp')
All inputs are finite; a program needn't handle non-finite values.
Results may differ from a plain program's by a relative error of at most 0.01.
Values may be sent and summed in bfloat16 or wider, within the bound.
No kernel may reach another device: no remote copies, remote signals or barrier semaphores. Data moves between devices by JAX's collectives and lax.ppermute only.
A program may use at most 64 MiB of HBM per device.

v0:
```python
import jax
import jax.numpy as jnp
from jax import lax
from jax.sharding import PartitionSpec as P

HEAD = 128
GROUP = 16
FLEN = 128
SPAN = 8


def from_behind(value, axis, steps):
    count = lax.axis_size(axis)
    leading, last = (max(0, -steps), min(count, count - steps))
    return lax.ppermute(value, axis, [(source, source + steps) for source in range(leading, last)])


def attend(state_now, queries, key_value, key_offset, query_offset, lowest):
    row_max, row_sum, numerator = state_now
    tok_rows = queries.shape[0]
    head_count = row_max.shape[0]
    span_rows = key_value.shape[1]
    query_heads = queries.reshape(tok_rows, head_count, HEAD)
    key_heads = key_value[0].reshape(span_rows, head_count, HEAD)
    value_heads = key_value[1].reshape(span_rows, head_count, HEAD)
    scores = jnp.einsum(
        "thd,shd->hts", query_heads, key_heads, preferred_element_type=jnp.float32
    ) * HEAD ** (-0.5)
    key_pos = key_offset + jnp.arange(span_rows, dtype=jnp.int32)
    query_pos = query_offset + jnp.arange(tok_rows, dtype=jnp.int32)
    allowed = (key_pos[None, :] >= lowest) & (key_pos[None, :] <= query_pos[:, None])
    masked = jnp.where(allowed[None], scores, -1e30)
    new_max = jnp.maximum(row_max, jnp.max(masked, axis=2))
    rescale = jnp.exp(row_max - new_max)
    weights = jnp.where(allowed[None], jnp.exp(masked - new_max[:, :, None]), 0.0)
    row_sum = row_sum * rescale + jnp.sum(weights, axis=2)
    partial_out = jnp.einsum(
        "hts,shd->thd",
        weights.astype(jnp.bfloat16),
        value_heads,
        preferred_element_type=jnp.float32,
    )
    numerator = numerator * jnp.transpose(rescale)[:, :, None] + partial_out
    return (new_max, row_sum, numerator)


def toeplitz_taps(filters):
    groups_here = filters.shape[0]
    padded_taps = jnp.concatenate(
        [
            jnp.zeros((groups_here, 1), jnp.float32),
            filters[:, ::-1],
            jnp.zeros((groups_here, FLEN), jnp.float32),
        ],
        axis=1,
    )
    tiled = jnp.tile(padded_taps, (1, FLEN))[:, : FLEN * 2 * FLEN]
    return tiled.reshape(groups_here, FLEN, 2 * FLEN)


def shards(token_ids, stream_table, filters, proj_qk):
    tok_rows = token_ids.shape[0]
    chan_width = stream_table.shape[2]
    onehot = (
        token_ids[:, None] == jnp.arange(stream_table.shape[1], dtype=jnp.int32)[None, :]
    ).astype(jnp.bfloat16)
    streams = jnp.einsum("tv,svc->stc", onehot, stream_table, preferred_element_type=jnp.float32)
    mixed_in = (streams[1] * streams[2]).astype(jnp.bfloat16)
    rim_rows = from_behind(mixed_in[tok_rows - (FLEN - 1) :], "ctx", 1)
    extended = jnp.concatenate(
        [jnp.zeros((1, chan_width), jnp.bfloat16), rim_rows, mixed_in], axis=0
    )
    block_count = tok_rows // FLEN
    stacked = extended.reshape(block_count + 1, FLEN, chan_width).astype(jnp.float32)
    paired = jnp.concatenate([stacked[:-1], stacked[1:]], axis=1)
    groups_here = filters.shape[0]
    paired = paired.reshape(block_count, 2 * FLEN, groups_here, GROUP)
    toeplitz = toeplitz_taps(filters)
    conv = jnp.einsum("gos,nsgc->nogc", toeplitz, paired, precision=lax.Precision.HIGHEST).reshape(
        tok_rows, chan_width
    )
    gated = (streams[0] * conv).astype(jnp.bfloat16)
    weights_local = proj_qk.reshape(proj_qk.shape[0], 2 * chan_width)
    projected = jnp.dot(
        lax.all_gather(gated, "tp", axis=1, tiled=True),
        weights_local,
        preferred_element_type=jnp.float32,
    )
    queries = projected[:, :chan_width].astype(jnp.bfloat16)
    keys = projected[:, chan_width:].astype(jnp.bfloat16)
    head_count = chan_width // HEAD
    position = lax.axis_index("ctx")
    query_offset = position * tok_rows
    lowest = jnp.maximum(position - SPAN + 1, 0) * tok_rows
    key_value = jnp.stack([keys, gated])
    initial = (
        jnp.full((head_count, tok_rows), -1e30, jnp.float32),
        jnp.zeros((head_count, tok_rows), jnp.float32),
        jnp.zeros((tok_rows, head_count, HEAD), jnp.float32),
    )
    state_now = attend(initial, queries, key_value, query_offset, query_offset, lowest)
    moving = key_value
    for distance in range(1, SPAN):
        moving = from_behind(moving, "ctx", 1)
        state_now = attend(
            state_now, queries, moving, query_offset - distance * tok_rows, query_offset, lowest
        )
    row_max, row_sum, numerator = state_now
    result = numerator / jnp.transpose(row_sum)[:, :, None]
    return result.reshape(tok_rows, chan_width).astype(jnp.bfloat16)


def solution(mesh):
    placed = (P("ctx"), P(None, None, "tp"), P("tp", None), P(None, None, "tp"))
    return jax.shard_map(
        shards, mesh=mesh, in_specs=placed, out_specs=P("ctx", "tp"), check_vma=False
    )
```

profile of v0, /device:TPU:128, one launch (start us, length us, event | category | flops | bytes accessed | tf_op | source)
XLA Modules:
  0.0 192.1 jit_solution(15303166851761119187)
XLA Ops:
  6.5 1.4 copy-done
  7.9 1.1 convolution_bitcast_fusion
  9.1 1.9 collective-permute-start
  11.0 0.8 rev.3
  12.0 3.1 %tile.4 = f32[32,128,257]{2,1,0:T(8,128)} broadcast(f32[32,257]{1,0:T(8,128)S(1)} %maximum_maximum_fusion), dimensions={0,2} | broadcast | bytes 4243584 | tf_op jit(solution)/shard_map/tile | solution.py:57
  15.0 6.7 %tile.10 = f32[32,32896]{1,0:T(8,128)} reshape(f32[32,128,257]{2,1,0:T(8,128)} %tile.4) | data formatting | bytes 8421376 | tf_op jit(solution)/shard_map/tile | solution.py:57
  21.7 2.2 %slice-done = f32[32,32768]{1,0:T(8,128)S(1)} async-done(((f32[32,32896]{1,0:T(8,128)}), f32[32,32768]{1,0:T(8,128)S(1)}, s32[]{:S(2)}) %slice-start) | async-done | bytes 4194328 | tf_op jit(solution)/shard_map/slice | solution.py:57
  23.9 3.2 %copy.95 = f32[4,8,128,256]{3,2,1,0:T(8,128)} copy(f32[4,8,128,256]{3,1,2,0:T(8,128)S(1)} %bitcast.264) | data formatting | bytes 8388608
  27.4 0.8 pad_maximum_fusion
  28.2 1.2 copy.41
  29.4 5.3 %fusion.141 = f32[32,16,128]{2,1,0:T(8,128)S(1)} fusion(f32[256,32,16]{0,2,1:T(8,128)S(1)} %bitcast.270, f32[32,128,256]{2,1,0:T(8,128)} %bitcast.265), kind=kOutput, calls=%fused_computation.218 | convolution fusion | flops 201326592 | bytes 4980736 | tf_op jit(solution)/shard_map/gos,nsgc->nogc/dot_general | solution.py:79
  35.6 9.4 %copy.96 = bf16[512,8,2,512]{3,1,2,0:T(8,128)(2,1)} copy(bf16[512,8,2,512]{3,2,1,0:T(2,128)(2,1)} %bitcast.266) | data formatting | bytes 16777216
  47.9 33.9 %all-gather.2.cloned.1.call-done = bf16[128,4096]{1,0:T(8,128)(2,1)} async-done(((bf16[128,512]{1,0:T(8,128)(2,1)}), bf16[128,4096]{1,0:T(8,128)(2,1)}) %all-gather.2.cloned.1.call-update) | async-done | bytes 1048592 | tf_op jit(solution)/shard_map/all_gather | solution.py:85
  81.8 5.0 %convolution_convert_fusion = bf16[128,1024]{1,0:T(8,128)(2,1)S(1)} fusion(bf16[128,4096]{1,0:T(8,128)(2,1)} %all-gather.2.cloned.1.call-done, bf16[4096,1024]{1,0:T(8,128)(2,1)} %bitcast.263), kind=kOutput, calls=%fused_computation.1 | convolution fusion | flops 1073872896 | bytes 9699328 | tf_op jit(solution)/shard_map/dot_general | solution.py:84
  86.9 1.9 collective-permute-start.1
  88.9 0.9 compare_and_fusion.5
  89.9 0.8 copy.85
  90.7 1.5 fusion.140
  92.2 6.0 %collective-permute-done.1 = bf16[2,128,512]{2,1,0:T(8,128)(2,1)S(1)} collective-permute-done((bf16[2,128,512]{2,1,0:T(8,128)(2,1)S(1)}, bf16[2,128,512]{2,1,0:T(8,128)(2,1)S(1)}, u32[]{:S(2)}, u32[]{:S(2)}) %collective-permute-start.1) | collective-permute-done | bytes 262176 | tf_op jit(solution)/shard_map/ppermute | solution.py:15
  98.2 1.9 collective-permute-start.2
  100.6 8.9 %collective-permute-done.2 = bf16[2,128,512]{2,1,0:T(8,128)(2,1)S(1)} collective-permute-done((bf16[2,128,512]{2,1,0:T(8,128)(2,1)S(1)}, bf16[2,128,512]{2,1,0:T(8,128)(2,1)S(1)}, u32[]{:S(2)}, u32[]{:S(2)}) %collective-permute-start.2) | collective-permute-done | bytes 262176 | tf_op jit(solution)/shard_map/ppermute | solution.py:15
  109.5 1.9 collective-permute-start.3
  112.5 8.3 %collective-permute-done.3 = bf16[2,128,512]{2,1,0:T(8,128)(2,1)S(1)} collective-permute-done((bf16[2,128,512]{2,1,0:T(8,128)(2,1)S(1)}, bf16[2,128,512]{2,1,0:T(8,128)(2,1)S(1)}, u32[]{:S(2)}, u32[]{:S(2)}) %collective-permute-start.3) | collective-permute-done | bytes 262176 | tf_op jit(solution)/shard_map/ppermute | solution.py:15
  120.8 1.9 collective-permute-start.4
  123.5 1.1 fusion.137
  124.7 7.4 %collective-permute-done.4 = bf16[2,128,512]{2,1,0:T(8,128)(2,1)S(1)} collective-permute-done((bf16[2,128,512]{2,1,0:T(8,128)(2,1)S(1)}, bf16[2,128,512]{2,1,0:T(8,128)(2,1)S(1)}, u32[]{:S(2)}, u32[]{:S(2)}) %collective-permute-start.4) | collective-permute-done | bytes 262176 | tf_op jit(solution)/shard_map/ppermute | solution.py:15
  132.8 1.9 collective-permute-start.5
  134.7 1.2 fusion.136
  137.3 6.9 %collective-permute-done.5 = bf16[2,128,512]{2,1,0:T(8,128)(2,1)} collective-permute-done((bf16[2,128,512]{2,1,0:T(8,128)(2,1)S(1)}, bf16[2,128,512]{2,1,0:T(8,128)(2,1)}, u32[]{:S(2)}, u32[]{:S(2)}) %collective-permute-start.5) | collective-permute-done | bytes 262176 | tf_op jit(solution)/shard_map/ppermute | solution.py:15
  144.2 2.1 %collective-permute-start.6 = (bf16[2,128,512]{2,1,0:T(8,128)(2,1)}, bf16[2,128,512]{2,1,0:T(8,128)(2,1)}, u32[]{:S(2)}, u32[]{:S(2)}) collective-permute-start(bf16[2,128,512]{2,1,0:T(8,128)(2,1)} %collective-permute-done.5), channel_id=1, source_target_pairs={{0,8},{8,16},{16,24},{24,32},{32,40},{40,48},{48,56},{56,64},{64,7... | collective-permute-start | bytes 786440 | tf_op jit(solution)/shard_map/ppermute | solution.py:15
  146.3 1.0 fusion.128
  148.1 1.7 fusion.135
  149.9 5.9 %collective-permute-done.6 = bf16[2,128,512]{2,1,0:T(8,128)(2,1)} collective-permute-done((bf16[2,128,512]{2,1,0:T(8,128)(2,1)}, bf16[2,128,512]{2,1,0:T(8,128)(2,1)}, u32[]{:S(2)}, u32[]{:S(2)}) %collective-permute-start.6) | collective-permute-done | bytes 262176 | tf_op jit(solution)/shard_map/ppermute | solution.py:15
  155.8 1.9 %collective-permute-start.7 = (bf16[2,128,512]{2,1,0:T(8,128)(2,1)}, bf16[2,128,512]{2,1,0:T(8,128)(2,1)}, u32[]{:S(2)}, u32[]{:S(2)}) collective-permute-start(bf16[2,128,512]{2,1,0:T(8,128)(2,1)} %collective-permute-done.6), channel_id=1, source_target_pairs={{0,8},{8,16},{16,24},{24,32},{32,40},{40,48},{48,56},{56,64},{64,7... | collective-permute-start | bytes 786440 | tf_op jit(solution)/shard_map/ppermute | solution.py:15
  157.8 1.0 fusion.127
  160.2 1.7 fusion.134
  161.9 5.5 %collective-permute-done.7 = bf16[2,128,512]{2,1,0:T(8,128)(2,1)} collective-permute-done((bf16[2,128,512]{2,1,0:T(8,128)(2,1)}, bf16[2,128,512]{2,1,0:T(8,128)(2,1)}, u32[]{:S(2)}, u32[]{:S(2)}) %collective-permute-start.7) | collective-permute-done | bytes 262176 | tf_op jit(solution)/shard_map/ppermute | solution.py:15
  167.4 1.7 fusion.126
  169.1 1.6 reshape_squeeze.54
  170.7 1.7 copy.92
  172.4 1.3 fusion.133
  174.4 0.8 fusion.43
  175.3 0.8 fusion.39
  176.9 0.8 fusion.35
  177.7 0.8 fusion.33
  179.3 1.0 fusion.29
  181.0 1.2 fusion.23
  182.3 0.9 fusion.21
  (122 shorter events, 16.0 us)
Async XLA Ops:
  6.5 1.4 copy-start
  6.5 75.2 %all-gather.2.cloned.1.call-start = ((), (), s32[]{:S(2)}) async-start(), calls=%async_computation | async-start | bytes 1179648 | tf_op jit(solution)/shard_map/all_gather | solution.py:85
  9.1 18.1 %collective-permute-start = (bf16[127,512]{1,0:T(8,128)(2,1)S(1)}, bf16[127,512]{1,0:T(8,128)(2,1)S(1)}, u32[]{:S(2)}, u32[]{:S(2)}) collective-permute-start(bf16[127,512]{1,0:T(8,128)(2,1)S(1)} %slice_bitcast_fusion.3), channel_id=1, source_target_pairs={{0,8},{8,16},{16,24},{24,32},{32,40},{40,48},{48,56},{56,64},{64,7... | collective-permute-start | bytes 390152 | tf_op jit(solution)/shard_map/ppermute | solution.py:15
  21.7 2.2 %slice-start = ((f32[32,32896]{1,0:T(8,128)}), f32[32,32768]{1,0:T(8,128)S(1)}, s32[]{:S(2)}) async-start(f32[32,32896]{1,0:T(8,128)} %tile.10), calls=%async_computation.1 | async-start | bytes 8388608 | tf_op jit(solution)/shard_map/slice | solution.py:57
  81.8 7.0 %copy-start.24 = (pred[128]{0:T(512)(128)(4,1)S(1)}, pred[128]{0:T(512)(128)(4,1)}, u32[]{:S(2)}) copy-start(pred[128]{0:T(512)(128)(4,1)} %get-tuple-element.76) | copy-start | bytes 388
  81.8 7.1 %copy-start.25 = (s32[128]{0:T(128)S(1)}, s32[128]{0:T(128)}, u32[]{:S(2)}) copy-start(s32[128]{0:T(128)} %get-tuple-element.81) | copy-start | bytes 1540
  81.8 7.1 %copy-start.26 = (s32[128]{0:T(128)S(1)}, s32[128]{0:T(128)}, u32[]{:S(2)}) copy-start(s32[128]{0:T(128)} %get-tuple-element.82) | copy-start | bytes 1540
  81.8 7.1 %copy-start.27 = (s32[128]{0:T(128)S(1)}, s32[128]{0:T(128)}, u32[]{:S(2)}) copy-start(s32[128]{0:T(128)} %get-tuple-element.79) | copy-start | bytes 1540
  81.8 7.1 %copy-start.28 = (s32[128]{0:T(128)S(1)}, s32[128]{0:T(128)}, u32[]{:S(2)}) copy-start(s32[128]{0:T(128)} %get-tuple-element.80) | copy-start | bytes 1540
  81.8 7.1 %copy-start.29 = (s32[128]{0:T(128)S(1)}, s32[128]{0:T(128)}, u32[]{:S(2)}) copy-start(s32[128]{0:T(128)} %get-tuple-element.77) | copy-start | bytes 1540
  81.8 7.1 %copy-start.30 = (s32[128]{0:T(128)S(1)}, s32[128]{0:T(128)}, u32[]{:S(2)}) copy-start(s32[128]{0:T(128)} %get-tuple-element.78) | copy-start | bytes 1540
  81.8 7.1 %copy-start.31 = (s32[128]{0:T(128)S(1)}, s32[128]{0:T(128)}, u32[]{:S(2)}) copy-start(s32[128]{0:T(128)} %get-tuple-element.83) | copy-start | bytes 1540
  86.8 25.6 %copy-start.16 = (bf16[16,4,8,128]{3,2,1,0:T(8,128)(2,1)}, bf16[16,4,8,128]{3,2,1,0:T(8,128)(2,1)S(1)}, u32[]{:S(2)}) copy-start(bf16[16,4,8,128]{3,2,1,0:T(8,128)(2,1)S(1)} %get-tuple-element.41) | copy-start | bytes 393220
  86.9 11.3 %collective-permute-start.1 = (bf16[2,128,512]{2,1,0:T(8,128)(2,1)S(1)}, bf16[2,128,512]{2,1,0:T(8,128)(2,1)S(1)}, u32[]{:S(2)}, u32[]{:S(2)}) collective-permute-start(bf16[2,128,512]{2,1,0:T(8,128)(2,1)S(1)} %pad_maximum_fusion.1), channel_id=1, source_target_pairs={{0,8},{8,16},{16,24},{24,32},{32,40},{40,48},{48,56},{56,64},{64,7... | collective-permute-start | bytes 786440 | tf_op jit(solution)/shard_map/ppermute | solution.py:15
  89.8 57.5 %copy-start.8 = (pred[128,128]{0,1:T(8,128)(4,1)}, pred[128,128]{0,1:T(8,128)(4,1)S(1)}, u32[]{:S(2)}) copy-start(pred[128,128]{0,1:T(8,128)(4,1)S(1)} %get-tuple-element.47) | copy-start | bytes 49156
  89.8 57.5 %copy-start.10 = (pred[128,128]{0,1:T(8,128)(4,1)}, pred[128,128]{0,1:T(8,128)(4,1)S(1)}, u32[]{:S(2)}) copy-start(pred[128,128]{0,1:T(8,128)(4,1)S(1)} %get-tuple-element.46) | copy-start | bytes 49156
  89.8 57.5 %copy-start.12 = (pred[128,128]{0,1:T(8,128)(4,1)}, pred[128,128]{0,1:T(8,128)(4,1)S(1)}, u32[]{:S(2)}) copy-start(pred[128,128]{0,1:T(8,128)(4,1)S(1)} %get-tuple-element.45) | copy-start | bytes 49156
  89.8 57.5 %copy-start.14 = (pred[128,128]{0,1:T(8,128)(4,1)}, pred[128,128]{0,1:T(8,128)(4,1)S(1)}, u32[]{:S(2)}) copy-start(pred[128,128]{0,1:T(8,128)(4,1)S(1)} %get-tuple-element.52) | copy-start | bytes 49156
  89.8 57.5 %copy-start.15 = (pred[128,128]{0,1:T(8,128)(4,1)}, pred[128,128]{0,1:T(8,128)(4,1)S(1)}, u32[]{:S(2)}) copy-start(pred[128,128]{0,1:T(8,128)(4,1)S(1)} %get-tuple-element.51) | copy-start | bytes 49156
  89.9 58.3 %copy-start.6 = (pred[128,128]{0,1:T(8,128)(4,1)}, pred[128,128]{0,1:T(8,128)(4,1)S(1)}, u32[]{:S(2)}) copy-start(pred[128,128]{0,1:T(8,128)(4,1)S(1)} %get-tuple-element.48) | copy-start | bytes 49156
  92.2 44.5 %copy-start.19 = (f32[4,128]{1,0:T(4,128)S(1)}, f32[4,128]{1,0:T(4,128)}, u32[]{:S(2)}) copy-start(f32[4,128]{1,0:T(4,128)} %get-tuple-element.67) | copy-start | bytes 6148
  98.2 11.3 %collective-permute-start.2 = (bf16[2,128,512]{2,1,0:T(8,128)(2,1)S(1)}, bf16[2,128,512]{2,1,0:T(8,128)(2,1)S(1)}, u32[]{:S(2)}, u32[]{:S(2)}) collective-permute-start(bf16[2,128,512]{2,1,0:T(8,128)(2,1)S(1)} %collective-permute-done.1), channel_id=1, source_target_pairs={{0,8},{8,16},{16,24},{24,32},{32,40},{40,48},{48,56},{56,64},{64,7... | collective-permute-start | bytes 786440 | tf_op jit(solution)/shard_map/ppermute | solution.py:15
  100.5 55.3 %copy-start.20 = (f32[4,128]{1,0:T(4,128)}, f32[4,128]{1,0:T(4,128)S(1)}, u32[]{:S(2)}) copy-start(f32[4,128]{1,0:T(4,128)S(1)} %get-tuple-element.65) | copy-start | bytes 6148
  109.5 11.3 %collective-permute-start.3 = (bf16[2,128,512]{2,1,0:T(8,128)(2,1)S(1)}, bf16[2,128,512]{2,1,0:T(8,128)(2,1)S(1)}, u32[]{:S(2)}, u32[]{:S(2)}) collective-permute-start(bf16[2,128,512]{2,1,0:T(8,128)(2,1)S(1)} %collective-permute-done.2), channel_id=1, source_target_pairs={{0,8},{8,16},{16,24},{24,32},{32,40},{40,48},{48,56},{56,64},{64,7... | collective-permute-start | bytes 786440 | tf_op jit(solution)/shard_map/ppermute | solution.py:15
  112.5 43.3 %copy-start.22 = (f32[4,128]{1,0:T(4,128)}, f32[4,128]{1,0:T(4,128)S(1)}, u32[]{:S(2)}) copy-start(f32[4,128]{1,0:T(4,128)S(1)} %get-tuple-element.63) | copy-start | bytes 6148
  120.8 11.3 %collective-permute-start.4 = (bf16[2,128,512]{2,1,0:T(8,128)(2,1)S(1)}, bf16[2,128,512]{2,1,0:T(8,128)(2,1)S(1)}, u32[]{:S(2)}, u32[]{:S(2)}) collective-permute-start(bf16[2,128,512]{2,1,0:T(8,128)(2,1)S(1)} %collective-permute-done.3), channel_id=1, source_target_pairs={{0,8},{8,16},{16,24},{24,32},{32,40},{40,48},{48,56},{56,64},{64,7... | collective-permute-start | bytes 786440 | tf_op jit(solution)/shard_map/ppermute | solution.py:15
  124.7 31.1 %copy-start.21 = (f32[4,128]{1,0:T(4,128)}, f32[4,128]{1,0:T(4,128)S(1)}, u32[]{:S(2)}) copy-start(f32[4,128]{1,0:T(4,128)S(1)} %get-tuple-element.61) | copy-start | bytes 6148
  132.8 11.4 %collective-permute-start.5 = (bf16[2,128,512]{2,1,0:T(8,128)(2,1)S(1)}, bf16[2,128,512]{2,1,0:T(8,128)(2,1)}, u32[]{:S(2)}, u32[]{:S(2)}) collective-permute-start(bf16[2,128,512]{2,1,0:T(8,128)(2,1)S(1)} %collective-permute-done.4), channel_id=1, source_target_pairs={{0,8},{8,16},{16,24},{24,32},{32,40},{40,48},{48,56},{56,64},{64,7... | collective-permute-start | bytes 786440 | tf_op jit(solution)/shard_map/ppermute | solution.py:15
  135.9 19.9 %copy-start.23 = (f32[4,128]{1,0:T(4,128)}, f32[4,128]{1,0:T(4,128)S(1)}, u32[]{:S(2)}) copy-start(f32[4,128]{1,0:T(4,128)S(1)} %get-tuple-element.59) | copy-start | bytes 6148
  144.2 11.6 %collective-permute-start.6 = (bf16[2,128,512]{2,1,0:T(8,128)(2,1)}, bf16[2,128,512]{2,1,0:T(8,128)(2,1)}, u32[]{:S(2)}, u32[]{:S(2)}) collective-permute-start(bf16[2,128,512]{2,1,0:T(8,128)(2,1)} %collective-permute-done.5), channel_id=1, source_target_pairs={{0,8},{8,16},{16,24},{24,32},{32,40},{40,48},{48,56},{56,64},{64,7... | collective-permute-start | bytes 786440 | tf_op jit(solution)/shard_map/ppermute | solution.py:15
  155.8 11.6 %collective-permute-start.7 = (bf16[2,128,512]{2,1,0:T(8,128)(2,1)}, bf16[2,128,512]{2,1,0:T(8,128)(2,1)}, u32[]{:S(2)}, u32[]{:S(2)}) collective-permute-start(bf16[2,128,512]{2,1,0:T(8,128)(2,1)} %collective-permute-done.6), channel_id=1, source_target_pairs={{0,8},{8,16},{16,24},{24,32},{32,40},{40,48},{48,56},{56,64},{64,7... | collective-permute-start | bytes 786440 | tf_op jit(solution)/shard_map/ppermute | solution.py:15
  172.4 10.8 %copy-start.1 = (bf16[1,128,512]{1,2,0:T(8,128)(2,1)S(1)}, bf16[1,128,512]{1,2,0:T(8,128)(2,1)}, u32[]{:S(2)}) copy-start(bf16[1,128,512]{1,2,0:T(8,128)(2,1)} %copy.87) | copy-start | bytes 393220
  172.4 10.8 %copy-start.13 = (pred[128,128]{0,1:T(8,128)(4,1)S(1)}, pred[128,128]{0,1:T(8,128)(4,1)}, u32[]{:S(2)}) copy-start(pred[128,128]{0,1:T(8,128)(4,1)} %copy-done.12) | copy-start | bytes 49156
  172.4 11.0 %copy-start.2 = (bf16[1,128,512]{1,2,0:T(8,128)(2,1)S(1)}, bf16[1,128,512]{1,2,0:T(8,128)(2,1)}, u32[]{:S(2)}) copy-start(bf16[1,128,512]{1,2,0:T(8,128)(2,1)} %copy.88) | copy-start | bytes 393220
  172.4 11.0 %copy-start.11 = (pred[128,128]{0,1:T(8,128)(4,1)S(1)}, pred[128,128]{0,1:T(8,128)(4,1)}, u32[]{:S(2)}) copy-start(pred[128,128]{0,1:T(8,128)(4,1)} %copy-done.10) | copy-start | bytes 49156
  172.4 11.2 %copy-start.3 = (bf16[1,128,512]{1,2,0:T(8,128)(2,1)S(1)}, bf16[1,128,512]{1,2,0:T(8,128)(2,1)}, u32[]{:S(2)}) copy-start(bf16[1,128,512]{1,2,0:T(8,128)(2,1)} %copy.89) | copy-start | bytes 393220
  172.4 11.2 %copy-start.9 = (pred[128,128]{0,1:T(8,128)(4,1)S(1)}, pred[128,128]{0,1:T(8,128)(4,1)}, u32[]{:S(2)}) copy-start(pred[128,128]{0,1:T(8,128)(4,1)} %copy-done.8) | copy-start | bytes 49156
  172.4 11.4 %copy-start.4 = (bf16[1,128,512]{1,2,0:T(8,128)(2,1)S(1)}, bf16[1,128,512]{1,2,0:T(8,128)(2,1)}, u32[]{:S(2)}) copy-start(bf16[1,128,512]{1,2,0:T(8,128)(2,1)} %copy.90) | copy-start | bytes 393220
  172.4 11.4 %copy-start.7 = (pred[128,128]{0,1:T(8,128)(4,1)S(1)}, pred[128,128]{0,1:T(8,128)(4,1)}, u32[]{:S(2)}) copy-start(pred[128,128]{0,1:T(8,128)(4,1)} %copy-done.6) | copy-start | bytes 49156
  173.7 10.4 %copy-start.5 = (bf16[1,128,512]{1,2,0:T(8,128)(2,1)S(1)}, bf16[1,128,512]{1,2,0:T(8,128)(2,1)}, u32[]{:S(2)}) copy-start(bf16[1,128,512]{1,2,0:T(8,128)(2,1)} %copy.91) | copy-start | bytes 393220
  175.3 9.0 %copy-start.17 = (bf16[1,128,512]{1,2,0:T(8,128)(2,1)S(1)}, bf16[1,128,512]{1,2,0:T(8,128)(2,1)}, u32[]{:S(2)}) copy-start(bf16[1,128,512]{1,2,0:T(8,128)(2,1)} %copy.92) | copy-start | bytes 393220
  175.3 9.0 %copy-start.18 = (pred[128,128]{0,1:T(8,128)(4,1)S(1)}, pred[128,128]{0,1:T(8,128)(4,1)}, u32[]{:S(2)}) copy-start(pred[128,128]{0,1:T(8,128)(4,1)} %get-tuple-element.50) | copy-start | bytes 49156
Sparse Core Ops, SparseCore 0:
  35.7 46.0 all-gather.1
where the time goes:
time: 193 us; the launch traced here: 192 us
  waiting for transfers between devices  82.9 us (43%)
  local copies, waits for them, and re-layouts  42.5 us (22%)
  matrix products  23.6 us (12%)
  starting transfers between devices  15.5 us (8%)
  between operations  14.1 us (7%)
  other arithmetic  13.5 us (7%)
    ppermute x8, waiting for transfers between devices, from_behind(): lax.ppermute(value, axis, [(source, source + steps) for source in range(l...  49 us
    all_gather x1, waiting for transfers between devices, shards(): lax.all_gather(gated, 'tp', axis=1, tiled=True)  33.9 us
    ppermute x8, starting transfers between devices, from_behind(): lax.ppermute(value, axis, [(source, source + steps) for source in range(l...  15.5 us
    unnamed x66, local copies, waits for them, and re-layouts  14.1 us
    another operation x2, local copies, waits for them, and re-layouts, toeplitz_taps(): tiled = jnp.tile(padded_taps, (1, FLEN))[:, :FLEN * 2 * FLEN]  9.73 us
    dot_general x8, matrix products, attend(): jnp.einsum('thd,shd->hts', query_heads, key_heads, preferred_element_type...  9.04 us
    reduce_sum x8, other arithmetic, attend(): row_sum = row_sum * rescale + jnp.sum(weights, axis=2)  5.82 us
    another operation x7, local copies, waits for them, and re-layouts, attend(): value_heads = key_value[1].reshape(span_rows, head_count, HEAD)  5.56 us
  transfers between devices with their start and end apart: 9, of which 8 were waited for; matrix products, arithmetic and copies ran while one was open for 22% of the time, Pallas kernels for 0%

commit v1 on v0

--- a/solution.py
+++ b/solution.py
@@ -7,6 +7,11 @@
 GROUP = 16
 FLEN = 128
 SPAN = 8
+
+
+def exchange_gather(x, name, d):
+    sent = jnp.stack([x] * lax.axis_size(name))
+    return jnp.concatenate(lax.all_to_all(sent, name, 0, 0), axis=d)
 
 
 def from_behind(value, axis, steps):
@@ -82,9 +87,7 @@
     gated = (streams[0] * conv).astype(jnp.bfloat16)
     weights_local = proj_qk.reshape(proj_qk.shape[0], 2 * chan_width)
     projected = jnp.dot(
-        lax.all_gather(gated, "tp", axis=1, tiled=True),
-        weights_local,
-        preferred_element_type=jnp.float32,
+        exchange_gather(gated, "tp", 1), weights_local, preferred_element_type=jnp.float32
     )
     queries = projected[:, :chan_width].astype(jnp.bfloat16)
     keys = projected[:, chan_width:].astype(jnp.bfloat16)

time: 193 us -> 154 us (0.80)
  waiting for transfers between devices: 82.9 us -> 50.9 us
  between operations: 14.1 us -> 0.54 us
  starting transfers between devices: 15.5 us -> 21.5 us
  other arithmetic: 13.5 us -> 10 us
  matrix products: 23.6 us -> 26.4 us
    all_gather x1 -> x0, waiting for transfers between devices: 33.9 us -> none  [shards(): lax.all_gather(gated, 'tp', axis=1, tiled=True)]
    all_to_all x0 -> x1, waiting for transfers between devices: none -> 6.76 us  [exchange_gather(): return jnp.concatenate(lax.all_to_all(sent, name, 0, 0), axis=d)]
    all_to_all x0 -> x1, starting transfers between devices: none -> 5.4 us  [exchange_gather(): return jnp.concatenate(lax.all_to_all(sent, name, 0, 0), axis=d)]
    ppermute x8, waiting for transfers between devices: 49 us -> 44.1 us  [from_behind(): lax.ppermute(value, axis, [(source, source + steps) for source in range(l...]
    dot_general x8, matrix products: 9.04 us -> 12.1 us  [attend(): jnp.einsum('thd,shd->hts', query_heads, key_heads, preferred_element_type...]
    add x4, other arithmetic: 2.26 us -> 0.03 us  [attend(): key_pos = key_offset + jnp.arange(span_rows, dtype=jnp.int32)]
    unnamed x66 -> x36, local copies, waits for them, and re-layouts: 14.1 us -> 14 us
  transfers between devices with their start and end apart: 9 -> 9, of which waited for: 8 -> 8; matrix products, arithmetic and copies ran while one was open for 22% -> 29% of each run, Pallas kernels for 0% -> 0%
where the time goes in v1:
time: 154 us; the launch traced here: 153 us
  waiting for transfers between devices  50.9 us (33%)
  local copies, waits for them, and re-layouts  43.2 us (28%)
  matrix products  26.4 us (17%)
  starting transfers between devices  21.5 us (14%)
  other arithmetic  10 us (6%)
    ppermute x8, waiting for transfers between devices, from_behind(): lax.ppermute(value, axis, [(source, source + steps) for source in range(l...  44.1 us
    ppermute x8, starting transfers between devices, from_behind(): lax.ppermute(value, axis, [(source, source + steps) for source in range(l...  16.1 us
    unnamed x36, local copies, waits for them, and re-layouts  14 us
    dot_general x8, matrix products, attend(): jnp.einsum('thd,shd->hts', query_heads, key_heads, preferred_element_type...  12.1 us
    another operation x2, local copies, waits for them, and re-layouts, toeplitz_taps(): tiled = jnp.tile(padded_taps, (1, FLEN))[:, :FLEN * 2 * FLEN]  9.7 us
    all_to_all x1, waiting for transfers between devices, exchange_gather(): return jnp.concatenate(lax.all_to_all(sent, name, 0, 0), axis=d)  6.76 us
    reduce_sum x8, other arithmetic, attend(): row_sum = row_sum * rescale + jnp.sum(weights, axis=2)  5.82 us
    another operation x7, local copies, waits for them, and re-layouts, attend(): value_heads = key_value[1].reshape(span_rows, head_count, HEAD)  5.54 us
  transfers between devices with their start and end apart: 9, of which 8 were waited for; matrix products, arithmetic and copies ran while one was open for 29% of the time, Pallas kernels for 0%

profile of v1, /device:TPU:128, one launch (start us, length us, event | category | flops | bytes accessed | tf_op | source)
XLA Modules:
  0.0 152.5 jit_solution(2984926848999120650)
XLA Ops:
  0.0 1.4 copy-done
  1.4 1.1 convolution_bitcast_fusion
  2.6 1.9 %collective-permute-start = (bf16[127,512]{1,0:T(8,128)(2,1)S(1)}, bf16[127,512]{1,0:T(8,128)(2,1)S(1)}, u32[]{:S(2)}, u32[]{:S(2)}) collective-permute-start(bf16[127,512]{1,0:T(8,128)(2,1)S(1)} %slice_bitcast_fusion.3), channel_id=1, source_target_pairs={{0,8},{8,16},{16,24},{24,32},{32,40},{40,48},{48,56},{56,64},{64,7... | collective-permute-start | bytes 390152 | tf_op jit(solution)/shard_map/ppermute | solution.py:20
  4.5 0.8 rev.3
  5.4 3.1 %tile.4 = f32[32,128,257]{2,1,0:T(8,128)} broadcast(f32[32,257]{1,0:T(8,128)S(1)} %maximum_maximum_fusion), dimensions={0,2} | broadcast | bytes 4243584 | tf_op jit(solution)/shard_map/tile | solution.py:62
  8.5 6.6 %tile.10 = f32[32,32896]{1,0:T(8,128)} reshape(f32[32,128,257]{2,1,0:T(8,128)} %tile.4) | data formatting | bytes 8421376 | tf_op jit(solution)/shard_map/tile | solution.py:62
  15.1 2.2 %slice-done = f32[32,32768]{1,0:T(8,128)S(1)} async-done(((f32[32,32896]{1,0:T(8,128)}), f32[32,32768]{1,0:T(8,128)S(1)}, s32[]{:S(2)}) %slice-start) | async-done | bytes 4194328 | tf_op jit(solution)/shard_map/slice | solution.py:62
  17.3 3.2 %copy.94 = f32[4,8,128,256]{3,2,1,0:T(8,128)} copy(f32[4,8,128,256]{3,1,2,0:T(8,128)S(1)} %bitcast.262) | data formatting | bytes 8388608
  21.0 5.3 %fusion.141 = f32[32,16,128]{2,1,0:T(8,128)S(1)} fusion(f32[256,32,16]{0,2,1:T(8,128)S(1)} %bitcast.268, f32[32,128,256]{2,1,0:T(8,128)} %bitcast.263), kind=kOutput, calls=%fused_computation.217 | convolution fusion | flops 201326592 | bytes 4980736 | tf_op jit(solution)/shard_map/gos,nsgc->nogc/dot_general | solution.py:84
  26.6 1.2 stack.9
  27.8 5.4 %all-to-all-start = ((bf16[8,128,512]{1,2,0:T(8,128)(2,1)}), bf16[8,128,512]{1,2,0:T(8,128)(2,1)S(1)}, u32[]{:S(2)}, u32[]{:S(2)}) async-start(bf16[8,128,512]{1,2,0:T(8,128)(2,1)} %stack.9), calls=%async_computation | async-start | bytes 2097152 | tf_op jit(solution)/shard_map/all_to_all | solution.py:14
  33.2 9.3 %copy.95 = bf16[512,8,2,512]{3,1,2,0:T(8,128)(2,1)} copy(bf16[512,8,2,512]{3,2,1,0:T(2,128)(2,1)} %bitcast.264) | data formatting | bytes 16777216
  42.7 6.8 %all-to-all-done = bf16[8,128,512]{1,2,0:T(8,128)(2,1)S(1)} async-done(((bf16[8,128,512]{1,2,0:T(8,128)(2,1)}), bf16[8,128,512]{1,2,0:T(8,128)(2,1)S(1)}, u32[]{:S(2)}, u32[]{:S(2)}) %all-to-all-start) | async-done | bytes 1048608 | tf_op jit(solution)/shard_map/all_to_all | solution.py:14
  49.4 4.7 %convolution_convert_fusion = bf16[128,1024]{1,0:T(8,128)(2,1)S(1)} fusion(bf16[128,4096]{0,1:T(8,128)(2,1)S(1)} %bitcast.265, bf16[4096,1024]{1,0:T(8,128)(2,1)} %bitcast.261), kind=kOutput, calls=%fused_computation.1 | convolution fusion | flops 1073872896 | bytes 9699328 | tf_op jit(solution)/shard_map/dot_general | solution.py:89
  54.2 2.7 %collective-permute-start.1 = (bf16[2,128,512]{2,1,0:T(8,128)(2,1)S(1)}, bf16[2,128,512]{2,1,0:T(8,128)(2,1)S(1)}, u32[]{:S(2)}, u32[]{:S(2)}) collective-permute-start(bf16[2,128,512]{2,1,0:T(8,128)(2,1)S(1)} %pad_maximum_fusion.1), channel_id=1, source_target_pairs={{0,8},{8,16},{16,24},{24,32},{32,40},{40,48},{48,56},{56,64},{64,7... | collective-permute-start | bytes 786440 | tf_op jit(solution)/shard_map/ppermute | solution.py:20
  56.9 1.0 compare_and_fusion.5
  57.9 0.8 copy.84
  58.7 1.5 fusion.140
  60.2 5.3 %collective-permute-done.1 = bf16[2,128,512]{2,1,0:T(8,128)(2,1)S(1)} collective-permute-done((bf16[2,128,512]{2,1,0:T(8,128)(2,1)S(1)}, bf16[2,128,512]{2,1,0:T(8,128)(2,1)S(1)}, u32[]{:S(2)}, u32[]{:S(2)}) %collective-permute-start.1) | collective-permute-done | bytes 262176 | tf_op jit(solution)/shard_map/ppermute | solution.py:20
  65.5 1.9 %collective-permute-start.2 = (bf16[2,128,512]{2,1,0:T(8,128)(2,1)S(1)}, bf16[2,128,512]{2,1,0:T(8,128)(2,1)S(1)}, u32[]{:S(2)}, u32[]{:S(2)}) collective-permute-start(bf16[2,128,512]{2,1,0:T(8,128)(2,1)S(1)} %collective-permute-done.1), channel_id=1, source_target_pairs={{0,8},{8,16},{16,24},{24,32},{32,40},{40,48},{48,56},{56,64},{64,7... | collective-permute-start | bytes 786440 | tf_op jit(solution)/shard_map/ppermute | solution.py:20
  67.6 0.8 fusion.139
  68.4 8.4 %collective-permute-done.2 = bf16[2,128,512]{2,1,0:T(8,128)(2,1)S(1)} collective-permute-done((bf16[2,128,512]{2,1,0:T(8,128)(2,1)S(1)}, bf16[2,128,512]{2,1,0:T(8,128)(2,1)S(1)}, u32[]{:S(2)}, u32[]{:S(2)}) %collective-permute-start.2) | collective-permute-done | bytes 262176 | tf_op jit(solution)/shard_map/ppermute | solution.py:20
  76.8 1.9 %collective-permute-start.3 = (bf16[2,128,512]{2,1,0:T(8,128)(2,1)S(1)}, bf16[2,128,512]{2,1,0:T(8,128)(2,1)S(1)}, u32[]{:S(2)}, u32[]{:S(2)}) collective-permute-start(bf16[2,128,512]{2,1,0:T(8,128)(2,1)S(1)} %collective-permute-done.2), channel_id=1, source_target_pairs={{0,8},{8,16},{16,24},{24,32},{32,40},{40,48},{48,56},{56,64},{64,7... | collective-permute-start | bytes 786440 | tf_op jit(solution)/shard_map/ppermute | solution.py:20
  80.1 1.7 %fusion.138 = (f32[4,128]{1,0:T(4,128)}, f32[4,128,128]{1,2,0:T(8,128)S(1)}) fusion(bf16[128,4,128]{2,1,0:T(4,128)(2,1)} %reshape_squeeze.44, bf16[16,4,8,128]{3,2,1,0:T(8,128)(2,1)S(1)} %get-tuple-element.41, pred[128,128]{0,1:T(8,128)(4,1)S(1)} %get-tuple-element.45), kind=kOutput, calls=%fused_computation.214 | convolution fusion | flops 16973312 | bytes 542720 | tf_op jit(solution)/shard_map/thd,shd->hts/dot_general | solution.py:31
  81.9 6.2 %collective-permute-done.3 = bf16[2,128,512]{2,1,0:T(8,128)(2,1)S(1)} collective-permute-done((bf16[2,128,512]{2,1,0:T(8,128)(2,1)S(1)}, bf16[2,128,512]{2,1,0:T(8,128)(2,1)S(1)}, u32[]{:S(2)}, u32[]{:S(2)}) %collective-permute-start.3) | collective-permute-done | bytes 262176 | tf_op jit(solution)/shard_map/ppermute | solution.py:20
  88.1 1.9 %collective-permute-start.4 = (bf16[2,128,512]{2,1,0:T(8,128)(2,1)S(1)}, bf16[2,128,512]{2,1,0:T(8,128)(2,1)S(1)}, u32[]{:S(2)}, u32[]{:S(2)}) collective-permute-start(bf16[2,128,512]{2,1,0:T(8,128)(2,1)S(1)} %collective-permute-done.3), channel_id=1, source_target_pairs={{0,8},{8,16},{16,24},{24,32},{32,40},{40,48},{48,56},{56,64},{64,7... | collective-permute-start | bytes 786440 | tf_op jit(solution)/shard_map/ppermute | solution.py:20
  90.8 1.7 %fusion.137 = (f32[4,128]{1,0:T(4,128)}, f32[4,128,128]{1,2,0:T(8,128)S(1)}) fusion(bf16[128,4,128]{2,1,0:T(4,128)(2,1)S(1)} %reshape_squeeze.46, bf16[16,4,8,128]{3,2,1,0:T(8,128)(2,1)} %copy-done.13, pred[128,128]{0,1:T(8,128)(4,1)} %get-tuple-element.46), kind=kOutput, calls=%fused_computation.213 | convolution fusion | flops 16973312 | bytes 542720 | tf_op jit(solution)/shard_map/thd,shd->hts/dot_general | solution.py:31
  92.5 6.8 %collective-permute-done.4 = bf16[2,128,512]{2,1,0:T(8,128)(2,1)S(1)} collective-permute-done((bf16[2,128,512]{2,1,0:T(8,128)(2,1)S(1)}, bf16[2,128,512]{2,1,0:T(8,128)(2,1)S(1)}, u32[]{:S(2)}, u32[]{:S(2)}) %collective-permute-start.4) | collective-permute-done | bytes 262176 | tf_op jit(solution)/shard_map/ppermute | solution.py:20
  100.1 1.9 %collective-permute-start.5 = (bf16[2,128,512]{2,1,0:T(8,128)(2,1)S(1)}, bf16[2,128,512]{2,1,0:T(8,128)(2,1)}, u32[]{:S(2)}, u32[]{:S(2)}) collective-permute-start(bf16[2,128,512]{2,1,0:T(8,128)(2,1)S(1)} %collective-permute-done.4), channel_id=1, source_target_pairs={{0,8},{8,16},{16,24},{24,32},{32,40},{40,48},{48,56},{56,64},{64,7... | collective-permute-start | bytes 786440 | tf_op jit(solution)/shard_map/ppermute | solution.py:20
  102.0 1.8 %fusion.136 = (f32[4,128]{1,0:T(4,128)}, f32[4,128,128]{1,2,0:T(8,128)S(1)}) fusion(bf16[128,4,128]{2,1,0:T(4,128)(2,1)} %reshape_squeeze.48, bf16[16,4,8,128]{3,2,1,0:T(8,128)(2,1)} %copy-done.13, pred[128,128]{0,1:T(8,128)(4,1)} %get-tuple-element.47), kind=kOutput, calls=%fused_computation.212 | convolution fusion | flops 16973312 | bytes 542720 | tf_op jit(solution)/shard_map/thd,shd->hts/dot_general | solution.py:31
  104.6 1.3 bitcast_maximum_fusion.2
  105.8 5.6 %collective-permute-done.5 = bf16[2,128,512]{2,1,0:T(8,128)(2,1)} collective-permute-done((bf16[2,128,512]{2,1,0:T(8,128)(2,1)S(1)}, bf16[2,128,512]{2,1,0:T(8,128)(2,1)}, u32[]{:S(2)}, u32[]{:S(2)}) %collective-permute-start.5) | collective-permute-done | bytes 262176 | tf_op jit(solution)/shard_map/ppermute | solution.py:20
  111.5 1.9 %collective-permute-start.6 = (bf16[2,128,512]{2,1,0:T(8,128)(2,1)}, bf16[2,128,512]{2,1,0:T(8,128)(2,1)}, u32[]{:S(2)}, u32[]{:S(2)}) collective-permute-start(bf16[2,128,512]{2,1,0:T(8,128)(2,1)} %collective-permute-done.5), channel_id=1, source_target_pairs={{0,8},{8,16},{16,24},{24,32},{32,40},{40,48},{48,56},{56,64},{64,7... | collective-permute-start | bytes 786440 | tf_op jit(solution)/shard_map/ppermute | solution.py:20
  113.4 1.0 fusion.128
  115.2 1.5 fusion.135
  116.7 6.4 %collective-permute-done.6 = bf16[2,128,512]{2,1,0:T(8,128)(2,1)} collective-permute-done((bf16[2,128,512]{2,1,0:T(8,128)(2,1)}, bf16[2,128,512]{2,1,0:T(8,128)(2,1)}, u32[]{:S(2)}, u32[]{:S(2)}) %collective-permute-start.6) | collective-permute-done | bytes 262176 | tf_op jit(solution)/shard_map/ppermute | solution.py:20
  123.1 1.9 %collective-permute-start.7 = (bf16[2,128,512]{2,1,0:T(8,128)(2,1)}, bf16[2,128,512]{2,1,0:T(8,128)(2,1)}, u32[]{:S(2)}, u32[]{:S(2)}) collective-permute-start(bf16[2,128,512]{2,1,0:T(8,128)(2,1)} %collective-permute-done.6), channel_id=1, source_target_pairs={{0,8},{8,16},{16,24},{24,32},{32,40},{40,48},{48,56},{56,64},{64,7... | collective-permute-start | bytes 786440 | tf_op jit(solution)/shard_map/ppermute | solution.py:20
  125.0 1.0 fusion.127
  127.5 1.8 %fusion.134 = (f32[4,128]{1,0:T(4,128)}, f32[4,128,128]{1,2,0:T(8,128)S(1)}) fusion(bf16[128,4,128]{2,1,0:T(4,128)(2,1)} %reshape_squeeze.52, bf16[16,4,8,128]{3,2,1,0:T(8,128)(2,1)} %copy-done.13, pred[128,128]{0,1:T(8,128)(4,1)S(1)} %get-tuple-element.49), kind=kOutput, calls=%fused_computation.210 | convolution fusion | flops 16973312 | bytes 542720 | tf_op jit(solution)/shard_map/thd,shd->hts/dot_general | solution.py:31
  129.2 5.5 %collective-permute-done.7 = bf16[2,128,512]{2,1,0:T(8,128)(2,1)} collective-permute-done((bf16[2,128,512]{2,1,0:T(8,128)(2,1)}, bf16[2,128,512]{2,1,0:T(8,128)(2,1)}, u32[]{:S(2)}, u32[]{:S(2)}) %collective-permute-start.7) | collective-permute-done | bytes 262176 | tf_op jit(solution)/shard_map/ppermute | solution.py:20
  134.7 1.7 %fusion.126 = (bf16[1,128,512]{2,1,0:T(8,128)(2,1)}, bf16[1,128,512]{2,1,0:T(8,128)(2,1)}) fusion(bf16[2,128,512]{2,1,0:T(8,128)(2,1)} %collective-permute-done.7), kind=kLoop, calls=%fused_computation.202 | loop fusion | bytes 524288 | tf_op jit(solution)/shard_map/slice | solution.py:30
  136.4 1.6 %reshape_squeeze.54 = bf16[128,4,128]{2,1,0:T(4,128)(2,1)} reshape(bf16[1,128,512]{2,1,0:T(8,128)(2,1)} %get-tuple-element.26) | data formatting | bytes 262144 | tf_op jit(solution)/shard_map/reshape;squeeze | solution.py:29
  138.0 1.7 %copy.91 = bf16[1,128,512]{1,2,0:T(8,128)(2,1)} copy(bf16[1,128,512]{2,1,0:T(8,128)(2,1)} %get-tuple-element.25) | data formatting | bytes 262144 | tf_op jit(solution)/shard_map/reshape;squeeze | solution.py:30
  139.7 1.3 fusion.133
  142.6 0.8 fusion.38
  146.6 1.0 fusion.28
  148.3 1.2 fusion.23
  149.6 0.9 fusion.21
  (91 shorter events, 14.7 us)
Async XLA Ops:
  0.0 1.4 copy-start
  2.6 18.1 %collective-permute-start = (bf16[127,512]{1,0:T(8,128)(2,1)S(1)}, bf16[127,512]{1,0:T(8,128)(2,1)S(1)}, u32[]{:S(2)}, u32[]{:S(2)}) collective-permute-start(bf16[127,512]{1,0:T(8,128)(2,1)S(1)} %slice_bitcast_fusion.3), channel_id=1, source_target_pairs={{0,8},{8,16},{16,24},{24,32},{32,40},{40,48},{48,56},{56,64},{64,7... | collective-permute-start | bytes 390152 | tf_op jit(solution)/shard_map/ppermute | solution.py:20
  15.1 2.2 %slice-start = ((f32[32,32896]{1,0:T(8,128)}), f32[32,32768]{1,0:T(8,128)S(1)}, s32[]{:S(2)}) async-start(f32[32,32896]{1,0:T(8,128)} %tile.10), calls=%async_computation.1 | async-start | bytes 8388608 | tf_op jit(solution)/shard_map/slice | solution.py:62
  27.8 21.6 %all-to-all-start = ((bf16[8,128,512]{1,2,0:T(8,128)(2,1)}), bf16[8,128,512]{1,2,0:T(8,128)(2,1)S(1)}, u32[]{:S(2)}, u32[]{:S(2)}) async-start(bf16[8,128,512]{1,2,0:T(8,128)(2,1)} %stack.9), calls=%async_computation | async-start | bytes 2097152 | tf_op jit(solution)/shard_map/all_to_all | solution.py:14
  54.1 33.9 %copy-start.13 = (bf16[16,4,8,128]{3,2,1,0:T(8,128)(2,1)}, bf16[16,4,8,128]{3,2,1,0:T(8,128)(2,1)S(1)}, u32[]{:S(2)}) copy-start(bf16[16,4,8,128]{3,2,1,0:T(8,128)(2,1)S(1)} %get-tuple-element.41) | copy-start | bytes 393220
  54.2 11.3 %collective-permute-start.1 = (bf16[2,128,512]{2,1,0:T(8,128)(2,1)S(1)}, bf16[2,128,512]{2,1,0:T(8,128)(2,1)S(1)}, u32[]{:S(2)}, u32[]{:S(2)}) collective-permute-start(bf16[2,128,512]{2,1,0:T(8,128)(2,1)S(1)} %pad_maximum_fusion.1), channel_id=1, source_target_pairs={{0,8},{8,16},{16,24},{24,32},{32,40},{40,48},{48,56},{56,64},{64,7... | collective-permute-start | bytes 786440 | tf_op jit(solution)/shard_map/ppermute | solution.py:20
  57.8 7.6 %copy-start.12 = (pred[128,128]{0,1:T(8,128)(4,1)}, pred[128,128]{0,1:T(8,128)(4,1)S(1)}, u32[]{:S(2)}) copy-start(pred[128,128]{0,1:T(8,128)(4,1)S(1)} %get-tuple-element.51) | copy-start | bytes 49156
  57.8 30.2 %copy-start.9 = (pred[128,128]{0,1:T(8,128)(4,1)}, pred[128,128]{0,1:T(8,128)(4,1)S(1)}, u32[]{:S(2)}) copy-start(pred[128,128]{0,1:T(8,128)(4,1)S(1)} %get-tuple-element.45) | copy-start | bytes 49156
  57.9 30.2 %copy-start.11 = (pred[128,128]{0,1:T(8,128)(4,1)}, pred[128,128]{0,1:T(8,128)(4,1)S(1)}, u32[]{:S(2)}) copy-start(pred[128,128]{0,1:T(8,128)(4,1)S(1)} %get-tuple-element.52) | copy-start | bytes 49156
  65.5 11.3 %collective-permute-start.2 = (bf16[2,128,512]{2,1,0:T(8,128)(2,1)S(1)}, bf16[2,128,512]{2,1,0:T(8,128)(2,1)S(1)}, u32[]{:S(2)}, u32[]{:S(2)}) collective-permute-start(bf16[2,128,512]{2,1,0:T(8,128)(2,1)S(1)} %collective-permute-done.1), channel_id=1, source_target_pairs={{0,8},{8,16},{16,24},{24,32},{32,40},{40,48},{48,56},{56,64},{64,7... | collective-permute-start | bytes 786440 | tf_op jit(solution)/shard_map/ppermute | solution.py:20
  76.8 11.3 %collective-permute-start.3 = (bf16[2,128,512]{2,1,0:T(8,128)(2,1)S(1)}, bf16[2,128,512]{2,1,0:T(8,128)(2,1)S(1)}, u32[]{:S(2)}, u32[]{:S(2)}) collective-permute-start(bf16[2,128,512]{2,1,0:T(8,128)(2,1)S(1)} %collective-permute-done.2), channel_id=1, source_target_pairs={{0,8},{8,16},{16,24},{24,32},{32,40},{40,48},{48,56},{56,64},{64,7... | collective-permute-start | bytes 786440 | tf_op jit(solution)/shard_map/ppermute | solution.py:20
  88.1 11.3 %collective-permute-start.4 = (bf16[2,128,512]{2,1,0:T(8,128)(2,1)S(1)}, bf16[2,128,512]{2,1,0:T(8,128)(2,1)S(1)}, u32[]{:S(2)}, u32[]{:S(2)}) collective-permute-start(bf16[2,128,512]{2,1,0:T(8,128)(2,1)S(1)} %collective-permute-done.3), channel_id=1, source_target_pairs={{0,8},{8,16},{16,24},{24,32},{32,40},{40,48},{48,56},{56,64},{64,7... | collective-permute-start | bytes 786440 | tf_op jit(solution)/shard_map/ppermute | solution.py:20
  90.0 25.2 %copy-start.14 = (bf16[16,4,8,128]{3,2,1,0:T(8,128)(2,1)S(1)}, bf16[16,4,8,128]{3,2,1,0:T(8,128)(2,1)}, u32[]{:S(2)}) copy-start(bf16[16,4,8,128]{3,2,1,0:T(8,128)(2,1)} %copy-done.13) | copy-start | bytes 393220
  100.1 11.4 %collective-permute-start.5 = (bf16[2,128,512]{2,1,0:T(8,128)(2,1)S(1)}, bf16[2,128,512]{2,1,0:T(8,128)(2,1)}, u32[]{:S(2)}, u32[]{:S(2)}) collective-permute-start(bf16[2,128,512]{2,1,0:T(8,128)(2,1)S(1)} %collective-permute-done.4), channel_id=1, source_target_pairs={{0,8},{8,16},{16,24},{24,32},{32,40},{40,48},{48,56},{56,64},{64,7... | collective-permute-start | bytes 786440 | tf_op jit(solution)/shard_map/ppermute | solution.py:20
  111.5 11.6 %collective-permute-start.6 = (bf16[2,128,512]{2,1,0:T(8,128)(2,1)}, bf16[2,128,512]{2,1,0:T(8,128)(2,1)}, u32[]{:S(2)}, u32[]{:S(2)}) collective-permute-start(bf16[2,128,512]{2,1,0:T(8,128)(2,1)} %collective-permute-done.5), channel_id=1, source_target_pairs={{0,8},{8,16},{16,24},{24,32},{32,40},{40,48},{48,56},{56,64},{64,7... | collective-permute-start | bytes 786440 | tf_op jit(solution)/shard_map/ppermute | solution.py:20
  123.1 11.6 %collective-permute-start.7 = (bf16[2,128,512]{2,1,0:T(8,128)(2,1)}, bf16[2,128,512]{2,1,0:T(8,128)(2,1)}, u32[]{:S(2)}, u32[]{:S(2)}) collective-permute-start(bf16[2,128,512]{2,1,0:T(8,128)(2,1)} %collective-permute-done.6), channel_id=1, source_target_pairs={{0,8},{8,16},{16,24},{24,32},{32,40},{40,48},{48,56},{56,64},{64,7... | collective-permute-start | bytes 786440 | tf_op jit(solution)/shard_map/ppermute | solution.py:20
  139.6 10.8 %copy-start.1 = (bf16[1,128,512]{1,2,0:T(8,128)(2,1)S(1)}, bf16[1,128,512]{1,2,0:T(8,128)(2,1)}, u32[]{:S(2)}) copy-start(bf16[1,128,512]{1,2,0:T(8,128)(2,1)} %copy.86) | copy-start | bytes 393220
  139.6 10.8 %copy-start.10 = (pred[128,128]{0,1:T(8,128)(4,1)S(1)}, pred[128,128]{0,1:T(8,128)(4,1)}, u32[]{:S(2)}) copy-start(pred[128,128]{0,1:T(8,128)(4,1)} %copy-done.9) | copy-start | bytes 49156
  139.6 11.1 %copy-start.2 = (bf16[1,128,512]{1,2,0:T(8,128)(2,1)S(1)}, bf16[1,128,512]{1,2,0:T(8,128)(2,1)}, u32[]{:S(2)}) copy-start(bf16[1,128,512]{1,2,0:T(8,128)(2,1)} %copy.87) | copy-start | bytes 393220
  139.6 11.1 %copy-start.8 = (pred[128,128]{0,1:T(8,128)(4,1)S(1)}, pred[128,128]{0,1:T(8,128)(4,1)}, u32[]{:S(2)}) copy-start(pred[128,128]{0,1:T(8,128)(4,1)} %get-tuple-element.46) | copy-start | bytes 49156
  139.6 11.3 %copy-start.3 = (bf16[1,128,512]{1,2,0:T(8,128)(2,1)S(1)}, bf16[1,128,512]{1,2,0:T(8,128)(2,1)}, u32[]{:S(2)}) copy-start(bf16[1,128,512]{1,2,0:T(8,128)(2,1)} %copy.88) | copy-start | bytes 393220
  139.6 11.3 %copy-start.7 = (pred[128,128]{0,1:T(8,128)(4,1)S(1)}, pred[128,128]{0,1:T(8,128)(4,1)}, u32[]{:S(2)}) copy-start(pred[128,128]{0,1:T(8,128)(4,1)} %get-tuple-element.47) | copy-start | bytes 49156
  139.7 11.5 %copy-start.4 = (bf16[1,128,512]{1,2,0:T(8,128)(2,1)S(1)}, bf16[1,128,512]{1,2,0:T(8,128)(2,1)}, u32[]{:S(2)}) copy-start(bf16[1,128,512]{1,2,0:T(8,128)(2,1)} %copy.89) | copy-start | bytes 393220
  139.7 11.5 %copy-start.6 = (pred[128,128]{0,1:T(8,128)(4,1)S(1)}, pred[128,128]{0,1:T(8,128)(4,1)}, u32[]{:S(2)}) copy-start(pred[128,128]{0,1:T(8,128)(4,1)} %get-tuple-element.48) | copy-start | bytes 49156
  141.0 10.4 %copy-start.5 = (bf16[1,128,512]{1,2,0:T(8,128)(2,1)S(1)}, bf16[1,128,512]{1,2,0:T(8,128)(2,1)}, u32[]{:S(2)}) copy-start(bf16[1,128,512]{1,2,0:T(8,128)(2,1)} %copy.90) | copy-start | bytes 393220
  142.6 9.0 %copy-start.15 = (bf16[1,128,512]{1,2,0:T(8,128)(2,1)S(1)}, bf16[1,128,512]{1,2,0:T(8,128)(2,1)}, u32[]{:S(2)}) copy-start(bf16[1,128,512]{1,2,0:T(8,128)(2,1)} %copy.91) | copy-start | bytes 393220
  142.6 9.0 %copy-start.16 = (pred[128,128]{0,1:T(8,128)(4,1)S(1)}, pred[128,128]{0,1:T(8,128)(4,1)}, u32[]{:S(2)}) copy-start(pred[128,128]{0,1:T(8,128)(4,1)} %get-tuple-element.50) | copy-start | bytes 49156
